TPU v7x, 32 devices: a whole 2x2x4 slice. The times are simulated.
32 devices in a mesh: dp: 16 (over z, x, core), tensor: 2 (over y).
Axes of the slice: x: 2, y: 2, z: 4, core: 2. Of those that a mesh axis runs over, the one named last changes fastest.
Arguments:
- tokens: bfloat16 [16, 1568, 768], P('dp', 'tensor'), may hold values from -6 to 6
- cotangent: bfloat16 [16, 1568, 768], P('dp', 'tensor'), may hold values from -6 to 6
- time_attend: bfloat16 [768, 3, 768], P('dp', None, 'tensor'), may hold values from -0.21875 to 0.21875
- time_output: bfloat16 [768, 768], P('tensor', 'dp'), may hold values from -0.625 to 0.625
- time_mixing: bfloat16 [768, 768], P('dp'), may hold values from -0.21875 to 0.21875
- space_attend: bfloat16 [768, 3, 768], P('dp', None, 'tensor'), may hold values from -0.21875 to 0.21875
- space_output: bfloat16 [768, 768], P('tensor', 'dp'), may hold values from -0.875 to 0.875
- hidden_expand: bfloat16 [768, 3072], P('dp', 'tensor'), may hold values from -0.21875 to 0.21875
- hidden_reduce: bfloat16 [3072, 768], P('tensor', 'dp'), may hold values from -0.109375 to 0.109375
- norm_time: float32 [768], replicated, may hold values from 0.1 to 1.9
- norm_space: float32 [768], replicated, may hold values from 0.1 to 1.9
- norm_hidden: float32 [768], replicated, may hold values from 0.1 to 1.9
- timeattend_lower: bfloat16 [8, 768, 16], replicated, may hold values from -0.21875 to 0.21875
- timeattend_raise: bfloat16 [8, 16, 3, 768], replicated, may hold values from -1.5 to 1.5
- timeoutput_lower: bfloat16 [8, 768, 16], replicated, may hold values from -0.21875 to 0.21875
- timeoutput_raise: bfloat16 [8, 16, 768], replicated, may hold values from -1.5 to 1.5
- timemixing_lower: bfloat16 [8, 768, 16], replicated, may hold values from -0.21875 to 0.21875
- timemixing_raise: bfloat16 [8, 16, 768], replicated, may hold values from -1.5 to 1.5
- spaceattend_lower: bfloat16 [8, 768, 16], replicated, may hold values from -0.21875 to 0.21875
- spaceattend_raise: bfloat16 [8, 16, 3, 768], replicated, may hold values from -1.5 to 1.5
- spaceoutput_lower: bfloat16 [8, 768, 16], replicated, may hold values from -0.21875 to 0.21875
- spaceoutput_raise: bfloat16 [8, 16, 768], replicated, may hold values from -1.5 to 1.5
- expand_lower: bfloat16 [8, 768, 16], replicated, may hold values from -0.21875 to 0.21875
- expand_raise: bfloat16 [8, 16, 3072], replicated, may hold values from -1.5 to 1.5
- reduce_lower: bfloat16 [8, 3072, 16], replicated, may hold values from -0.109375 to 0.109375
- reduce_raise: bfloat16 [8, 16, 768], replicated, may hold values from -1.5 to 1.5
- adapter_index: int32 [16], P('dp'), may hold values from 0 to 7
- clip_mask: int32 [16], P('dp'), may hold values 0 or 1
Outputs:
- layer_output: bfloat16 [16, 1568, 768], P('dp', 'tensor')
- input_grad: bfloat16 [16, 1568, 768], P('dp', 'tensor')
- timeattend_lowgrad: float32 [8, 768, 16], replicated
- timeattend_raisegrad: float32 [8, 16, 3, 768], replicated
- timeoutput_lowgrad: float32 [8, 768, 16], replicated
- timeoutput_raisegrad: float32 [8, 16, 768], replicated
- timemixing_lowgrad: float32 [8, 768, 16], replicated
- timemixing_raisegrad: float32 [8, 16, 768], replicated
- spaceattend_lowgrad: float32 [8, 768, 16], replicated
- spaceattend_raisegrad: float32 [8, 16, 3, 768], replicated
- spaceoutput_lowgrad: float32 [8, 768, 16], replicated
- spaceoutput_raisegrad: float32 [8, 16, 768], replicated
- expand_lowgrad: float32 [8, 768, 16], replicated
- expand_raisegrad: float32 [8, 16, 3072], replicated
- reduce_lowgrad: float32 [8, 3072, 16], replicated
- reduce_raisegrad: float32 [8, 16, 768], replicated
All inputs are finite; a program needn't handle non-finite values. No bound on the sum of `clip_mask` on one device may be relied on, other than what follows from the above.
Results may differ from a plain program's by a relative error of at most 0.04.
Values may be sent and summed in bfloat16 or wider, within the bound.
No kernel may reach another device: no remote copies, remote signals or barrier semaphores. Data moves between devices by JAX's collectives and lax.ppermute only.
A program may use at most 256 MiB of HBM per device.

v0:
```python
from functools import partial

import jax
import jax.numpy as jnp
from jax import lax
from jax.sharding import PartitionSpec as P

HEAD = 64
PLACES = 196
BF = jnp.bfloat16
F32 = jnp.float32
ALL = ("dp", "tensor")
TIME_FORMS = ("fphe,gphe->phfg", "phfg,gphe->fphe", "phfg,fphe->gphe")
SPACE_FORMS = ("fphe,fqhe->fhpq", "fhpq,fqhe->fphe", "fhpq,fphe->fqhe")


def mm(a, b):
    return lax.dot_general(a, b, (((1,), (0,)), ((), ())), preferred_element_type=F32)


def mm_t(a, b):
    return lax.dot_general(a, b, (((1,), (1,)), ((), ())), preferred_element_type=F32)


def t_mm(a, b):
    return lax.dot_general(a, b, (((0,), (0,)), ((), ())), preferred_element_type=F32)


def layer_norm(values, gain):
    center = jnp.mean(values, axis=-1, keepdims=True)
    offset = values - center
    spread = jnp.mean(offset * offset, axis=-1, keepdims=True)
    return offset * lax.rsqrt(spread + 1e-06) * gain


def split_heads(packed, frames):
    rows, width = packed.shape
    shaped = packed.reshape(frames, rows // frames, 3, width // (3 * HEAD), HEAD)
    return (shaped[:, :, 0], shaped[:, :, 1], shaped[:, :, 2])


def attend(packed, frames, forms):
    query, keys, values = split_heads(packed, frames)
    scores = jnp.einsum(forms[0], query, keys, preferred_element_type=F32) * HEAD ** (-0.5)
    totals = jax.nn.logsumexp(scores, axis=-1, keepdims=True)
    weights = jnp.exp(scores - totals).astype(BF)
    mixed = jnp.einsum(forms[1], weights, values, preferred_element_type=F32)
    return (mixed.reshape(packed.shape[0], packed.shape[1] // 3), totals)


def attend_back(out_grad, packed, totals, frames, forms):
    query, keys, values = split_heads(packed, frames)
    grad = out_grad.reshape(query.shape)
    scale = HEAD ** (-0.5)
    scores = jnp.einsum(forms[0], query, keys, preferred_element_type=F32) * scale
    probs = jnp.exp(scores - totals)
    prob_grad = jnp.einsum(forms[0], grad, values, preferred_element_type=F32)
    value_grad = jnp.einsum(forms[2], probs.astype(BF), grad, preferred_element_type=F32)
    score_grad = probs * (prob_grad - jnp.sum(probs * prob_grad, axis=-1, keepdims=True))
    score_grad = score_grad.astype(BF)
    query_grad = jnp.einsum(forms[1], score_grad, keys, preferred_element_type=F32) * scale
    key_grad = jnp.einsum(forms[2], score_grad, query, preferred_element_type=F32) * scale
    stacked = jnp.stack((query_grad, key_grad, value_grad), axis=2)
    return stacked.reshape(packed.shape)


def body(
    tokens,
    cotangent,
    time_attend,
    time_output,
    time_mixing,
    space_attend,
    space_output,
    hidden_expand,
    hidden_reduce,
    norm_time,
    norm_space,
    norm_hidden,
    timeattend_lower,
    timeattend_raise,
    timeoutput_lower,
    timeoutput_raise,
    timemixing_lower,
    timemixing_raise,
    spaceattend_lower,
    spaceattend_raise,
    spaceoutput_lower,
    spaceoutput_raise,
    expand_lower,
    expand_raise,
    reduce_lower,
    reduce_raise,
    adapter_index,
    clip_mask,
    *,
    dp,
    tensor,
):
    me = lax.axis_index("tensor")
    devices = dp * tensor
    clips, length, width = tokens.shape
    frames = length // PLACES
    half = PLACES // tensor
    adapters, _, rank = timeattend_lower.shape
    cols = width // tensor
    units = hidden_expand.shape[1]
    adapter = adapter_index[0]
    valid = clip_mask[0].astype(F32)
    swap = [(i, (i + 1) % tensor) for i in range(tensor)]

    def slabs(matrix):
        rows = matrix.shape[0]
        return matrix.reshape(rows, -1, cols).transpose(1, 0, 2)

    mixing_cols = lax.dynamic_slice_in_dim(time_mixing, me * cols, cols, 1)
    time_pack = jnp.concatenate(
        [slabs(time_attend), slabs(time_output.T), slabs(mixing_cols)], axis=0
    )
    rest_pack = jnp.concatenate(
        [
            slabs(space_attend),
            slabs(space_output.T),
            slabs(hidden_expand),
            slabs(hidden_reduce.T),
        ],
        axis=0,
    )

    def gather(pack):
        whole = lax.all_gather(pack, ALL, axis=0, tiled=False)
        count, rows, _ = pack.shape
        whole = whole.reshape(dp, tensor, count, rows, cols).transpose(2, 0, 3, 1, 4)
        return whole.reshape(count, width, width)

    time_whole = gather(time_pack)
    rest_whole = gather(rest_pack)

    def wide(parts):
        return jnp.concatenate([parts[i] for i in range(parts.shape[0])], axis=1)

    def pick(table):
        picked = lax.dynamic_index_in_dim(table, adapter, 0, keepdims=False)
        if picked.ndim == 3:
            picked = picked.reshape(picked.shape[0], -1)
        return picked

    def regroup(table, axis):
        shape = table.shape
        pieces = units // cols
        split = shape[:axis] + (tensor, pieces, cols) + shape[axis + 1 :]
        return jnp.swapaxes(table.reshape(split), axis, axis + 1).reshape(shape)

    def ungroup(table, axis):
        shape = table.shape
        pieces = units // cols
        split = shape[:axis] + (pieces, tensor, cols) + shape[axis + 1 :]
        return jnp.swapaxes(table.reshape(split), axis, axis + 1).reshape(shape)

    def effective(weight, lower, raised):
        return (weight.astype(F32) + mm(lower, raised)).astype(BF)

    def effective_t(weight_t, lower, raised):
        update = lax.dot_general(
            raised, lower, (((0,), (1,)), ((), ())), preferred_element_type=F32
        )
        return (weight_t.astype(F32) + update).astype(BF)

    ta = (pick(timeattend_lower), pick(timeattend_raise))
    to = (pick(timeoutput_lower), pick(timeoutput_raise))
    tm = (pick(timemixing_lower), pick(timemixing_raise))
    sa = (pick(spaceattend_lower), pick(spaceattend_raise))
    so = (pick(spaceoutput_lower), pick(spaceoutput_raise))
    he = (pick(expand_lower), regroup(pick(expand_raise), 1))
    hr = (regroup(pick(reduce_lower), 0), pick(reduce_raise))

    w_ta = effective(wide(time_whole[0:3]), *ta)
    w_to = effective_t(time_whole[3], *to)
    w_tm = effective(time_whole[4], *tm)
    w_sa = effective(wide(rest_whole[0:3]), *sa)
    w_so = effective_t(rest_whole[3], *so)
    w_he = effective(wide(rest_whole[4:8]), *he)
    w_hr = effective_t(wide(rest_whole[8:12]), *hr)

    def low_rank(acts, grad, pair):
        inner = mm(acts, pair[0]).astype(BF)
        inner_grad = mm_t(grad, pair[1]).astype(BF)
        lower_grad = t_mm(inner_grad, acts)
        raised_grad = t_mm(inner, grad)
        return (lower_grad, raised_grad)

    def to_places(values):
        values = values.reshape(frames // tensor, PLACES, width)
        mine = lax.dynamic_slice_in_dim(values, me * half, half, 1)
        other = lax.dynamic_slice_in_dim(values, (1 - me) * half, half, 1)
        got = lax.ppermute(other, "tensor", swap)
        return jnp.concatenate([mine, got], axis=0).reshape(-1, width)

    def to_frames(values):
        values = values.reshape(frames, half, width)
        mine = values[: frames // tensor]
        got = lax.ppermute(values[frames // tensor :], "tensor", swap)
        first = jnp.where(me == 0, mine, got)
        second = jnp.where(me == 0, got, mine)
        return jnp.concatenate([first, second], axis=1).reshape(-1, width)

    frames = frames * tensor
    start = tokens[0].astype(F32)
    start_p = to_places(tokens[0]).astype(F32)
    normed_time = layer_norm(start_p, norm_time).astype(BF)
    packed_time = mm(normed_time, w_ta).astype(BF)
    heads_time, totals_time = attend(packed_time, frames, TIME_FORMS)
    heads_time = heads_time.astype(BF)
    merged_time = mm_t(heads_time, w_to).astype(BF)
    delta = to_frames(mm(merged_time, w_tm).astype(BF))
    local = frames // tensor
    after_time = start + delta.astype(F32)
    normed_space = layer_norm(after_time, norm_space).astype(BF)
    packed_space = mm(normed_space, w_sa).astype(BF)
    heads_space, totals_space = attend(packed_space, local, SPACE_FORMS)
    heads_space = heads_space.astype(BF)
    after_space = after_time + mm_t(heads_space, w_so)
    normed_hidden = layer_norm(after_space, norm_hidden).astype(BF)
    hidden = mm(normed_hidden, w_he)
    active = jax.nn.gelu(hidden, approximate=False).astype(BF)
    layer_output = ((after_space + mm_t(active, w_hr)) * valid).astype(BF)

    upstream = cotangent[0].astype(F32) * valid
    up_low = upstream.astype(BF)
    active_grad = mm(up_low, w_hr)
    g_hr = low_rank(active, up_low, hr)
    _, gelu_back = jax.vjp(partial(jax.nn.gelu, approximate=False), hidden)
    hidden_grad = gelu_back(active_grad)[0].astype(BF)
    g_he = low_rank(normed_hidden, hidden_grad, he)
    _, norm_back = jax.vjp(partial(layer_norm, gain=norm_hidden), after_space)
    space_grad = upstream + norm_back(mm_t(hidden_grad, w_he))[0]
    space_low = space_grad.astype(BF)
    g_so = low_rank(heads_space, space_low, so)
    heads_grad = mm(space_low, w_so).astype(BF)
    packed_grad = attend_back(heads_grad, packed_space, totals_space, local, SPACE_FORMS)
    packed_grad = packed_grad.astype(BF)
    g_sa = low_rank(normed_space, packed_grad, sa)
    _, norm_back = jax.vjp(partial(layer_norm, gain=norm_space), after_time)
    time_grad = space_grad + norm_back(mm_t(packed_grad, w_sa))[0]

    mixing_grad = to_places(time_grad.astype(BF))
    g_tm = low_rank(merged_time, mixing_grad, tm)
    merged_grad = mm_t(mixing_grad, w_tm).astype(BF)
    g_to = low_rank(heads_time, merged_grad, to)
    heads_grad = mm(merged_grad, w_to).astype(BF)
    packed_grad = attend_back(heads_grad, packed_time, totals_time, frames, TIME_FORMS)
    packed_grad = packed_grad.astype(BF)
    g_ta = low_rank(normed_time, packed_grad, ta)
    _, norm_back = jax.vjp(partial(layer_norm, gain=norm_time), start_p)
    first_grad = to_frames(norm_back(mm_t(packed_grad, w_ta))[0].astype(BF))
    input_grad = (time_grad + first_grad.astype(F32)).astype(BF)

    def reduce_tables(pieces):
        flat = jnp.concatenate([piece.astype(BF).reshape(-1) for piece in pieces])
        each = flat.size // devices
        label = jnp.full((devices, 128), adapter, jnp.int32).astype(BF)
        sent = jnp.concatenate([flat.reshape(devices, each), label], axis=1)
        got = lax.all_to_all(sent, ALL, 0, 0, tiled=True)
        owner = got[:, each : each + 1].astype(jnp.int32)
        choose = (owner == jnp.arange(adapters, dtype=jnp.int32)[None, :]).astype(BF)
        total = t_mm(choose, got[:, :each]).astype(BF)
        whole = lax.all_gather(total, ALL, axis=0, tiled=False)
        whole = whole.transpose(1, 0, 2).reshape(adapters, devices * each)
        parts = []
        at = 0
        for piece in pieces:
            parts.append(whole[:, at : at + piece.size].reshape((adapters,) + piece.shape))
            at += piece.size
        return [part.astype(F32) for part in parts]

    late = reduce_tables([*g_hr, *g_he, *g_so, *g_sa])
    early = reduce_tables([*g_tm, *g_to, *g_ta])

    def lowered(part):
        return jnp.swapaxes(part, 1, 2)

    def threes(part):
        return part.reshape(adapters, rank, 3, width)

    return (
        layer_output[None],
        input_grad[None],
        lowered(early[4]),
        threes(early[5]),
        lowered(early[2]),
        early[3],
        lowered(early[0]),
        early[1],
        lowered(late[6]),
        threes(late[7]),
        lowered(late[4]),
        late[5],
        lowered(late[2]),
        ungroup(late[3], 2),
        lowered(ungroup(late[0], 2)),
        late[1],
    )


def solution(mesh):
    whole = P()
    step = partial(body, dp=mesh.shape["dp"], tensor=mesh.shape["tensor"])
    return jax.shard_map(
        step,
        mesh=mesh,
        in_specs=(
            P("dp", "tensor", None),
            P("dp", "tensor", None),
            P("dp", None, "tensor"),
            P("tensor", "dp"),
            P("dp", None),
            P("dp", None, "tensor"),
            P("tensor", "dp"),
            P("dp", "tensor"),
            P("tensor", "dp"),
        )
        + (whole,) * 17
        + (P("dp"), P("dp")),
        out_specs=(P("dp", "tensor", None), P("dp", "tensor", None)) + (whole,) * 14,
        check_vma=False,
    )
```

profile of v0, /device:TPU:0, one launch (start us, length us, event | category | flops | bytes accessed | tf_op | source)
XLA Modules:
  0.0 751.0 jit_solution(14355740103799324401)
XLA Ops:
  20.5 13.2 %collective-permute-done = bf16[4,98,768]{2,0,1:T(4,128)(2,1)S(1)} collective-permute-done((bf16[4,98,768]{2,0,1:T(4,128)(2,1)S(1)}, bf16[4,98,768]{2,0,1:T(4,128)(2,1)S(1)}, u32[]{:S(2)}, u32[]{:S(2)}) %collective-permute-start) | collective-permute-done | bytes 602144 | tf_op jit(solution)/shard_map/ppermute | solution.py:196
  38.3 44.7 %all-gather.9.cloned.1.call-done = bf16[160,48,384]{2,1,0:T(8,128)(2,1)} async-done(((bf16[5,48,384]{2,1,0:T(8,128)(2,1)}), bf16[160,48,384]{2,1,0:T(8,128)(2,1)}) %all-gather.9.cloned.1.call-update) | async-done | bytes 5898256 | tf_op jit(solution)/shard_map/all_gather | solution.py:131
  83.0 9.0 %copy.481 = bf16[16,2,5,48,384]{4,1,3,0,2:T(2,128)(2,1)S(1)} copy(bf16[16,2,5,48,384]{4,3,2,1,0:T(8,128)(2,1)} %bitcast.441) | data formatting | bytes 11796480 | tf_op jit(solution)/shard_map/reshape | solution.py:133
  109.8 11.8 %reshape.597 = bf16[8,98,3,12,64]{4,3,2,1,0:T(8,128)(2,1)} reshape(bf16[784,2304]{1,0:T(8,128)(2,1)} %convolution_convert_fusion.2) | data formatting | bytes 7225344 | tf_op jit(solution)/shard_map/reshape | solution.py:38
  121.6 5.0 fusion.165
  158.0 23.3 %collective-permute-done.1 = bf16[4,98,768]{2,0,1:T(4,128)(2,1)} collective-permute-done((bf16[4,98,768]{2,0,1:T(4,128)(2,1)}, bf16[4,98,768]{2,0,1:T(4,128)(2,1)}, u32[]{:S(2)}, u32[]{:S(2)}) %collective-permute-start.1) | collective-permute-done | bytes 602144 | tf_op jit(solution)/shard_map/ppermute | solution.py:202
  188.6 13.1 %all-gather.11.cloned.1.call-done = bf16[384,48,384]{2,1,0:T(8,128)(2,1)} async-done(((bf16[12,48,384]{2,1,0:T(8,128)(2,1)}), bf16[384,48,384]{2,1,0:T(8,128)(2,1)}) %all-gather.11.cloned.1.call-update) | async-done | bytes 14155792 | tf_op jit(solution)/shard_map/all_gather | solution.py:131
  201.6 14.8 %fusion.163 = (bf16[1,16,48,2,384]{4,2,0,3,1:T(8,128)(2,1)S(1)}, bf16[1,16,48,2,384]{4,2,0,3,1:T(8,128)(2,1)S(1)}, bf16[1,16,48,2,384]{4,2,0,3,1:T(8,128)(2,1)S(...) fusion(bf16[12,16,48,2,384]{4,2,0,3,1:T(8,128)(2,1)} %bitcast.431), kind=kLoop, calls=%fused_computation.300 | loop fusion | flops 589824 | bytes 29491200 | tf_op jit(solution)/shard_map/slice | solution.py:140
  249.7 11.8 %reshape.598 = bf16[4,196,3,12,64]{4,3,2,1,0:T(8,128)(2,1)} reshape(bf16[784,2304]{1,0:T(8,128)(2,1)} %convolution_convert_fusion.1) | data formatting | bytes 7225344 | tf_op jit(solution)/shard_map/reshape | solution.py:38
  261.6 7.0 fusion.164
  278.3 5.2 copy.408
  310.7 25.7 %multiply_convert_fusion.1 = (bf16[784,3072]{1,0:T(8,128)(2,1)}, f32[784,3072]{1,0:T(8,128)}, f32[784,3072]{1,0:T(8,128)}) fusion(bf16[784,768]{1,0:T(8,128)(2,1)S(1)} %multiply_convert_fusion.5, bf16[768,3072]{1,0:T(8,128)(2,1)S(1)} %add_convert_fusion.2), kind=kOutput, calls=%fused_computation.7 | convolution fusion | flops 3855925248 | bytes 30007296 | tf_op jit(solution)/shard_map/dot_general | solution.py:18
  349.3 12.4 %add_convert_fusion = bf16[784,3072]{1,0:T(8,128)(2,1)S(1)} fusion(f32[784,3072]{1,0:T(8,128)} %get-tuple-element.119, f32[784,3072]{1,0:T(8,128)} %get-tuple-element.177, bf16[768,3072]{1,0:T(8,128)(2,1)S(1)} %add_convert_fusion.1, bf16[1,784,768]{2,1,0:T(8,128)(2,1)S(1)} %copy-done.8, f32[]{:T(128)} %bitcast.37), kind=kOutput, calls=%fused_computation.6 | convolution fusion | flops 3734900736 | bytes 30007300 | tf_op jit(solution)/shard_map/dot_general | solution.py:18
  363.9 7.9 %multiply_reduce_fusion.7 = (f32[784]{0:T(1024)S(1)}, f32[784,768]{1,0:T(8,128)}) fusion(f32[784,768]{1,0:T(8,128)S(1)} %copy-done.14, f32[768]{0:T(1024)S(1)} %copy-done.92, f32[784]{0:T(1024)S(1)} %copy-done.74, bf16[784,3072]{1,0:T(8,128)(2,1)S(1)} %add_convert_fusion, bf16[768,3072]{1,0:T(8,128)(2,1)} %copy-done.96), kind=kOutput, calls=%fused_computation.70 | convolution fusion | flops 3701783808 | bytes 14361728 | tf_op jit(solution)/shard_map/dot_general | solution.py:22
  403.3 7.5 convolution_bitcast_fusion
  410.8 7.8 %multiply_reduce_fusion = (f32[4,12,196]{2,1,0:T(8,128)S(1)}, f32[4,12,196,196]{2,3,1,0:T(8,128)}) fusion(f32[4,12,196,196]{2,3,1,0:T(8,128)} %copy-done.2, f32[4,12,196]{2,1,0:T(8,128)S(1)} %copy-done.47, bf16[4,196,12,64]{1,3,2,0:T(8,128)(2,1)S(1)} %copy-done.32, bf16[4,196,1,12,64]{1,4,3,0,2:T(8,128)(2,1)S(1)} %copy-done.31), kind=kOutput, calls=%fused_computation.2 | convolution fusion | flops 243394368 | bytes 17235456 | tf_op jit(solution)/shard_map/fphe,fqhe->fhpq/dot_general | solution.py:57
  418.6 11.5 %multiply_convert_fusion = bf16[4,12,196,196]{2,3,1,0:T(8,128)(2,1)} fusion(f32[4,12,196,196]{2,3,1,0:T(8,128)} %get-tuple-element.181, f32[4,12,196,196]{2,3,1,0:T(8,128)} %copy-done.2, f32[4,12,196]{2,1,0:T(8,128)S(1)} %get-tuple-element.180, f32[4,12,196]{2,1,0:T(8,128)S(1)} %copy-done.47), kind=kLoop, calls=%fused_computation.1 | loop fusion | flops 9219840 | bytes 18514944 | tf_op jit(solution)/shard_map/convert_element_type | solution.py:60
  437.4 6.6 copy.366
  444.0 9.7 %convert_element_type.470 = bf16[784,2304]{0,1:T(8,128)(2,1)} reshape(bf16[4,196,3,12,64]{1,0,4,3,2:T(4,128)(2,1)} %copy.366) | data formatting | bytes 7225344 | tf_op jit(solution)/shard_map/convert_element_type | solution.py:241
  453.7 8.9 %multiply_reduce_fusion.6 = (f32[784]{0:T(1024)S(1)}, f32[784,768]{1,0:T(8,128)}) fusion(f32[784,768]{1,0:T(8,128)} %copy-done.7, f32[768]{0:T(1024)S(1)} %copy-done.76, f32[784]{0:T(1024)S(1)} %copy-done.70, bf16[784,2304]{0,1:T(8,128)(2,1)} %convert_element_type.470, bf16[768,2304]{1,0:T(8,128)(2,1)} %copy-done.94), kind=kOutput, calls=%fused_computation.69 | convolution fusion | flops 2776939776 | bytes 11977856 | tf_op jit(solution)/shard_map/dot_general | solution.py:22
  467.4 5.0 convolution_convert_fusion.5
  482.6 14.1 %collective-permute-done.2 = bf16[4,98,768]{2,0,1:T(4,128)(2,1)S(1)} collective-permute-done((bf16[4,98,768]{2,0,1:T(4,128)(2,1)S(1)}, bf16[4,98,768]{2,0,1:T(4,128)(2,1)S(1)}, u32[]{:S(2)}, u32[]{:S(2)}) %collective-permute-start.2) | collective-permute-done | bytes 602144 | tf_op jit(solution)/shard_map/ppermute | solution.py:196
  517.0 6.7 fusion.18
  540.9 6.5 copy.373
  549.6 6.0 copy.372
  559.3 11.3 %copy.377 = bf16[8,98,3,12,64]{1,0,4,3,2:T(8,128)(2,1)} copy(bf16[8,98,3,12,64]{1,4,3,2,0:T(8,128)(2,1)S(1)} %maximum_convert_fusion.1) | data formatting | bytes 7225344 | tf_op jit(solution)/shard_map/convert_element_type | solution.py:252
  570.7 9.0 %convert_element_type.476 = bf16[784,2304]{0,1:T(8,128)(2,1)} reshape(bf16[8,98,3,12,64]{1,0,4,3,2:T(8,128)(2,1)} %copy.377) | data formatting | bytes 7225344 | tf_op jit(solution)/shard_map/convert_element_type | solution.py:252
  597.0 5.2 all-to-all-done
  607.0 7.0 multiply_reduce_fusion.5
  620.1 8.8 %fusion.32 = bf16[1,784,768]{2,1,0:T(8,128)(2,1)} fusion(f32[784,768]{1,0:T(8,128)S(1)} %copy-done.15, bf16[784,3072]{1,0:T(8,128)(2,1)} %get-tuple-element.118, bf16[768,3072]{1,0:T(8,128)(2,1)} %copy-done.95, f32[]{:T(128)} %bitcast.37), kind=kOutput, calls=%fused_computation.111 | convolution fusion | flops 3701182464 | bytes 13148164 | tf_op jit(solution)/shard_map/dot_general | solution.py:22
  645.0 21.1 %all-gather.13.cloned.1.call-done = bf16[256,3072]{1,0:T(8,128)(2,1)} async-done(((bf16[8,3072]{1,0:T(8,128)(2,1)}), bf16[256,3072]{1,0:T(8,128)(2,1)}) %all-gather.13.cloned.1.call-update) | async-done | bytes 1572880 | tf_op jit(solution)/shard_map/all_gather | solution.py:267
  674.4 53.0 %all-gather.15.cloned.1.call-done = bf16[256,6144]{1,0:T(8,128)(2,1)} async-done(((bf16[8,6144]{1,0:T(8,128)(2,1)}), bf16[256,6144]{1,0:T(8,128)(2,1)}) %all-gather.15.cloned.1.call-update) | async-done | bytes 3145744 | tf_op jit(solution)/shard_map/all_gather | solution.py:267
  (449 shorter events, 323.3 us)
Async XLA Ops:
  7.2 146.1 %copy-start = (bf16[8,16,3072]{2,1,0:T(8,128)(2,1)S(1)}, bf16[8,16,3072]{2,1,0:T(8,128)(2,1)}, u32[]{:S(2)}) copy-start(bf16[8,16,3072]{2,1,0:T(8,128)(2,1)} %param.51) | copy-start | bytes 2359300
  7.2 75.8 %all-gather.9.cloned.1.call-start = ((), (), s32[]{:S(2)}) async-start(), calls=%async_computation.2 | async-start | bytes 6082560 | tf_op jit(solution)/shard_map/all_gather | solution.py:131
  9.8 191.8 %all-gather.11.cloned.1.call-start = ((), (), s32[]{:S(2)}) async-start(), calls=%async_computation.3 | async-start | bytes 14598144 | tf_op jit(solution)/shard_map/all_gather | solution.py:131
  15.5 19.2 %copy-start.26 = (bf16[4,98,768]{2,1,0:T(8,128)(2,1)}, bf16[4,98,768]{2,1,0:T(8,128)(2,1)S(1)}, u32[]{:S(2)}) copy-start(bf16[4,98,768]{2,1,0:T(8,128)(2,1)S(1)} %get-tuple-element.163) | copy-start | bytes 1806340
  15.8 17.9 %collective-permute-start = (bf16[4,98,768]{2,0,1:T(4,128)(2,1)S(1)}, bf16[4,98,768]{2,0,1:T(4,128)(2,1)S(1)}, u32[]{:S(2)}, u32[]{:S(2)}) collective-permute-start(bf16[4,98,768]{2,0,1:T(4,128)(2,1)S(1)} %copy.323), channel_id=1, source_target_pairs={{0,1},{1,0},{2,3},{3,2},{4,5},{5,4},{6,7},{7,6},{8,9},{9,8},{10,11... | collective-permute-start | bytes 1806344 | tf_op jit(solution)/shard_map/ppermute | solution.py:196
  20.5 79.7 %copy-start.65 = (bf16[2,8,3,768]{3,1,2,0:T(8,128)(2,1)}, bf16[2,8,3,768]{3,1,2,0:T(8,128)(2,1)S(1)}, u32[]{:S(2)}) copy-start(bf16[2,8,3,768]{3,1,2,0:T(8,128)(2,1)S(1)} %copy.412) | copy-start | bytes 221188
  34.1 69.2 %copy-start.85 = (f32[784]{0:T(1024)}, f32[784]{0:T(1024)S(1)}, u32[]{:S(2)}) copy-start(f32[784]{0:T(1024)S(1)} %div.63) | copy-start | bytes 9412
  34.8 68.5 %copy-start.87 = (f32[784]{0:T(1024)}, f32[784]{0:T(1024)S(1)}, u32[]{:S(2)}) copy-start(f32[784]{0:T(1024)S(1)} %rsqrt.36) | copy-start | bytes 9412
  38.3 65.1 %copy-start.11 = (f32[784,768]{1,0:T(8,128)}, f32[784,768]{1,0:T(8,128)S(1)}, u32[]{:S(2)}) copy-start(f32[784,768]{1,0:T(8,128)S(1)} %reshape.563) | copy-start | bytes 7225348
  151.8 29.4 %collective-permute-start.1 = (bf16[4,98,768]{2,0,1:T(4,128)(2,1)}, bf16[4,98,768]{2,0,1:T(4,128)(2,1)}, u32[]{:S(2)}, u32[]{:S(2)}) collective-permute-start(bf16[4,98,768]{2,0,1:T(4,128)(2,1)} %copy.333), channel_id=1, source_target_pairs={{0,1},{1,0},{2,3},{3,2},{4,5},{5,4},{6,7},{7,6},{8,9},{9,8},{10,11... | collective-permute-start | bytes 1806344 | tf_op jit(solution)/shard_map/ppermute | solution.py:202
  154.2 150.5 %copy-start.62 = (bf16[16,3072]{1,0:T(8,128)(2,1)}, bf16[16,3072]{1,0:T(8,128)(2,1)S(1)}, u32[]{:S(2)}) copy-start(bf16[16,3072]{1,0:T(8,128)(2,1)S(1)} %reshape.534) | copy-start | bytes 294916
  156.0 84.2 %copy-start.67 = (bf16[2,8,3,768]{3,1,2,0:T(8,128)(2,1)}, bf16[2,8,3,768]{3,1,2,0:T(8,128)(2,1)S(1)}, u32[]{:S(2)}) copy-start(bf16[2,8,3,768]{3,1,2,0:T(8,128)(2,1)S(1)} %copy.418) | copy-start | bytes 221188
  188.1 113.6 %copy-start.7 = (f32[784,768]{1,0:T(8,128)}, f32[784,768]{1,0:T(8,128)S(1)}, u32[]{:S(2)}) copy-start(f32[784,768]{1,0:T(8,128)S(1)} %get-tuple-element.121) | copy-start | bytes 7225348
  188.1 55.3 %copy-start.69 = (f32[784]{0:T(1024)}, f32[784]{0:T(1024)S(1)}, u32[]{:S(2)}) copy-start(f32[784]{0:T(1024)S(1)} %broadcast_multiply_fusion.1) | copy-start | bytes 9412
  188.5 27.9 %copy-start.77 = (f32[784]{0:T(1024)}, f32[784]{0:T(1024)S(1)}, u32[]{:S(2)}) copy-start(f32[784]{0:T(1024)S(1)} %multiply_reduce_fusion.9) | copy-start | bytes 9412
  188.6 54.8 %copy-start.71 = (f32[784]{0:T(1024)}, f32[784]{0:T(1024)S(1)}, u32[]{:S(2)}) copy-start(f32[784]{0:T(1024)S(1)} %fusion.148) | copy-start | bytes 9412
  310.6 25.8 %copy-start.96 = (bf16[768,3072]{1,0:T(8,128)(2,1)}, bf16[768,3072]{1,0:T(8,128)(2,1)S(1)}, u32[]{:S(2)}) copy-start(bf16[768,3072]{1,0:T(8,128)(2,1)S(1)} %add_convert_fusion.2) | copy-start | bytes 14155780
  310.6 25.7 %copy-start.8 = (bf16[1,784,768]{2,1,0:T(8,128)(2,1)S(1)}, bf16[1,784,768]{2,1,0:T(8,128)(2,1)}, u32[]{:S(2)}) copy-start(bf16[1,784,768]{2,1,0:T(8,128)(2,1)} %param.29) | copy-start | bytes 3612676
  310.7 25.7 %copy-start.64 = (bf16[3072,16]{0,1:T(8,128)(2,1)S(1)}, bf16[3072,16]{0,1:T(8,128)(2,1)}, u32[]{:S(2)}) copy-start(bf16[3072,16]{0,1:T(8,128)(2,1)} %reshape.536) | copy-start | bytes 294916
  349.3 12.4 %copy-start.95 = (bf16[768,3072]{1,0:T(8,128)(2,1)}, bf16[768,3072]{1,0:T(8,128)(2,1)S(1)}, u32[]{:S(2)}) copy-start(bf16[768,3072]{1,0:T(8,128)(2,1)S(1)} %add_convert_fusion.1) | copy-start | bytes 14155780
  349.3 14.6 %copy-start.14 = (f32[784,768]{1,0:T(8,128)S(1)}, f32[784,768]{1,0:T(8,128)}, u32[]{:S(2)}) copy-start(f32[784,768]{1,0:T(8,128)} %copy-done.13) | copy-start | bytes 7225348
  349.3 14.6 %copy-start.74 = (f32[784]{0:T(1024)S(1)}, f32[784]{0:T(1024)}, u32[]{:S(2)}) copy-start(f32[784]{0:T(1024)} %copy-done.73) | copy-start | bytes 9412
  349.3 14.5 %copy-start.92 = (f32[768]{0:T(1024)S(1)}, f32[768]{0:T(1024)}, u32[]{:S(2)}) copy-start(f32[768]{0:T(1024)} %param.39) | copy-start | bytes 9220
  383.2 92.7 %copy-start.5 = (f32[784,768]{1,0:T(8,128)}, f32[784,768]{1,0:T(8,128)S(1)}, u32[]{:S(2)}) copy-start(f32[784,768]{1,0:T(8,128)S(1)} %get-tuple-element.117) | copy-start | bytes 7225348
  444.0 9.7 %copy-start.76 = (f32[768]{0:T(1024)S(1)}, f32[768]{0:T(1024)}, u32[]{:S(2)}) copy-start(f32[768]{0:T(1024)} %param.38) | copy-start | bytes 9220
  480.9 15.8 %collective-permute-start.2 = (bf16[4,98,768]{2,0,1:T(4,128)(2,1)S(1)}, bf16[4,98,768]{2,0,1:T(4,128)(2,1)S(1)}, u32[]{:S(2)}, u32[]{:S(2)}) collective-permute-start(bf16[4,98,768]{2,0,1:T(4,128)(2,1)S(1)} %copy.367), channel_id=1, source_target_pairs={{0,1},{1,0},{2,3},{3,2},{4,5},{5,4},{6,7},{7,6},{8,9},{9,8},{10,11... | collective-permute-start | bytes 1806344 | tf_op jit(solution)/shard_map/ppermute | solution.py:196
  512.0 11.7 %slice-start = ((s8[4816896]{0:T(1024)(128)(4,1)}), s8[622592]{0:T(1024)(128)(4,1)S(1)}, s32[]{:S(2)}) async-start(s8[4816896]{0:T(1024)(128)(4,1)} %bitcast.428), calls=%async_computation.6 | async-start | bytes 1245184
  589.5 12.7 %all-to-all-start = ((bf16[32,2,1600]{2,1,0:T(2,128)(2,1)}), bf16[32,2,1600]{2,1,0:T(2,128)(2,1)S(1)}, u32[]{:S(2)}, u32[]{:S(2)}) async-start(bf16[32,2,1600]{2,1,0:T(2,128)(2,1)} %reshape.603), calls=%async_computation | async-start | bytes 425984 | tf_op jit(solution)/shard_map/all_to_all | solution.py:263
  602.2 27.9 %all-to-all-start.1 = ((bf16[32,2,3136]{2,1,0:T(2,128)(2,1)}), bf16[32,2,3136]{2,1,0:T(2,128)(2,1)}, u32[]{:S(2)}, u32[]{:S(2)}) async-start(bf16[32,2,3136]{2,1,0:T(2,128)(2,1)} %reshape.605), calls=%async_computation.1 | async-start | bytes 819200 | tf_op jit(solution)/shard_map/all_to_all | solution.py:263
  605.5 60.6 %all-gather.13.cloned.1.call-start = ((), (), s32[]{:S(2)}) async-start(), calls=%async_computation.4 | async-start | bytes 1622016 | tf_op jit(solution)/shard_map/all_gather | solution.py:267
  606.9 120.5 %all-gather.15.cloned.1.call-start = ((), (), s32[]{:S(2)}) async-start(), calls=%async_computation.5 | async-start | bytes 3244032 | tf_op jit(solution)/shard_map/all_gather | solution.py:267
  618.6 16.2 %collective-permute-start.3 = (bf16[4,98,768]{2,0,1:T(4,128)(2,1)}, bf16[4,98,768]{2,0,1:T(4,128)(2,1)}, u32[]{:S(2)}, u32[]{:S(2)}) collective-permute-start(bf16[4,98,768]{2,0,1:T(4,128)(2,1)} %copy.378), channel_id=1, source_target_pairs={{0,1},{1,0},{2,3},{3,2},{4,5},{5,4},{6,7},{7,6},{8,9},{9,8},{10,11... | collective-permute-start | bytes 1806344 | tf_op jit(solution)/shard_map/ppermute | solution.py:202
  (77 other events, 317.7 us)
Sparse Core Ops, SparseCore 0:
  11.5 71.4 all-gather.8
  86.5 115.0 all-gather.10
  609.8 56.2 all-gather.12
  669.4 57.9 all-gather.14
where the time goes:
time: 758 us; the launch traced here: 751 us
  local copies, waits for them, and re-layouts  241 us (32%)
  matrix products  212 us (28%)
  waiting for transfers between devices  188 us (25%)
  other arithmetic  79.7 us (11%)
  between operations  17.2 us (2%)
  starting transfers between devices  12.9 us (2%)
    all_gather x2, waiting for transfers between devices, reduce_tables(): whole = lax.all_gather(total, ALL, axis=0, tiled=False)  74.1 us
    dot_general x11, matrix products, mm(): lax.dot_general(a, b, (((1,), (0,)), ((), ())), preferred_element_type=F32)  69.9 us
    unnamed x253, local copies, waits for them, and re-layouts  65.2 us
    all_gather x2, waiting for transfers between devices, gather(): whole = lax.all_gather(pack, ALL, axis=0, tiled=False)  57.8 us
    dot_general x16, matrix products, t_mm(): lax.dot_general(a, b, (((0,), (0,)), ((), ())), preferred_element_type=F32)  45.9 us
    dot_general x7, matrix products, mm_t(): lax.dot_general(a, b, (((1,), (1,)), ((), ())), preferred_element_type=F32)  38.8 us
    convert_element_type x4, local copies, waits for them, and re-layouts, body(): packed_grad = packed_grad.astype(BF)  36.7 us
    ppermute x2, waiting for transfers between devices, to_places(): got = lax.ppermute(other, 'tensor', swap)  27.3 us
  transfers between devices with their start and end apart: 10, of which 9 were waited for; matrix products, arithmetic and copies ran while one was open for 18% of the time, Pallas kernels for 0%

commit v1 on v0

v1 whole, which is shorter than its diff:
```python
from functools import partial
import jax
import jax.numpy as jnp
from jax import lax
from jax.experimental import pallas as pl
from jax.experimental.pallas import tpu as pltpu
from jax.sharding import PartitionSpec as P

BF = jnp.bfloat16
F32 = jnp.float32
HEAD = 64
PLACES = 196
LOW = -1e30


def mm(a, b):
    return lax.dot_general(a, b, (((1,), (0,)), ((), ())), preferred_element_type=F32)


def mm_t(a, b):
    return lax.dot_general(a, b, (((1,), (1,)), ((), ())), preferred_element_type=F32)


def t_mm(a, b):
    return lax.dot_general(a, b, (((0,), (0,)), ((), ())), preferred_element_type=F32)


def norm_parts(x):
    center = jnp.mean(x, axis=-1, keepdims=True)
    offset = x - center
    spread = jnp.mean(offset * offset, axis=-1, keepdims=True)
    root = lax.rsqrt(spread + 1e-06)
    return (offset * root, root)


def norm_back(grad, x, gain):
    unit, root = norm_parts(x)
    grad = grad * gain
    first = jnp.mean(grad, axis=-1, keepdims=True)
    second = jnp.mean(grad * unit, axis=-1, keepdims=True)
    return root * (grad - first - unit * second)


def two_heads(x):
    lane = lax.broadcasted_iota(jnp.int32, x.shape, 1)
    zero = jnp.zeros_like(x)
    return jnp.concatenate([jnp.where(lane < HEAD, x, zero), jnp.where(lane < HEAD, zero, x)], axis=0)


def one_pair(x):
    size = x.shape[0] // 2
    lane = lax.broadcasted_iota(jnp.int32, (size, x.shape[1]), 1)
    return jnp.where(lane < HEAD, x[:size], x[size:])


def attend(query, keys, values, bias):
    size = keys.shape[0]
    scores = mm_t(two_heads(keys), query).reshape(2, size, size) + bias[None]
    top = jnp.max(scores, axis=1, keepdims=True)
    parts = jnp.exp(scores - top)
    total = jnp.sum(parts, axis=1, keepdims=True)
    probs = (parts * (1.0 / total)).reshape(2 * size, size).astype(BF)
    mixed = t_mm(two_heads(values), probs)
    return (probs, mixed.T.astype(BF))


def attend_back(grad, query, keys, values, probs):
    size = keys.shape[0]
    prob_grad = mm_t(two_heads(values), grad)
    value_grad = one_pair(mm(probs, grad))
    wide = probs.astype(F32)
    mass = wide * prob_grad
    total = jnp.sum(mass.reshape(2, size, size), axis=1, keepdims=True)
    score_grad = mass - (wide.reshape(2, size, size) * total).reshape(2 * size, size)
    score_grad = score_grad.astype(BF)
    key_grad = one_pair(mm(score_grad, query))
    query_grad = t_mm(two_heads(keys), score_grad).T * HEAD ** (-0.5)
    return (query_grad.astype(BF), key_grad.astype(BF), value_grad.astype(BF))


def split_lanes(ref, base, value):
    for lane in range(value.shape[-1] // 128):
        ref[base + lane] = value[..., lane * 128 : lane * 128 + 128]


def join_lanes(ref, base, count):
    return jnp.concatenate([ref[base + lane] for lane in range(count)], axis=-1)


def gelu_parts(hidden):
    cdf = 0.5 * (1.0 + lax.erf(hidden * 0.7071067811865476))
    density = jnp.exp(-0.5 * hidden * hidden) * 0.3989422804014327
    return (hidden * cdf, cdf + hidden * density)


def space_kernel(
    tokens, delta, cot, valid, gain_s, gain_h, units, gathered,
    out, tgrad, tlow, grads,
    w, x, up, ys, n_lo, qkv, dqkv, probs, att, acc, dacc, gacc, bias, sems,
    *, places, pad,
):
    step = pl.program_id(0)
    nd, nt, count, wr, wc = gathered.shape
    width = nt * wc
    chunk = tokens.shape[0]
    rows = chunk * pad
    lanes = width // 128

    def copies(s):
        return [
            pltpu.make_async_copy(
                gathered.at[:, t, s], w.at[s, :, :, pl.ds(t * wc, wc)], sems.at[s, t]
            )
            for t in range(nt)
        ]

    sides = [(0, 1), (0, 2), (0, 3), (5, 4)] + [(6, 7 + i) for i in range(4)] + [(15, 11 + i) for i in range(4)]

    def slab(s):
        return w[s].reshape(width, width)

    @pl.when(step == 0)
    def _():
        for s in range(count):
            for copy in copies(s):
                copy.start()
        x[:, places:, :] = jnp.zeros((chunk, pad - places, width), F32)
        up[:, places:, :] = jnp.zeros((chunk, pad - places, width), F32)
        key = lax.broadcasted_iota(jnp.int32, (pad, pad), 0)
        bias[...] = jnp.where(key < places, 0.0, LOW)
        gacc[...] = jnp.zeros_like(gacc)
        for s in range(count):
            for copy in copies(s):
                copy.wait()
            a, b = sides[s]
            new = slab(s).astype(F32) + t_mm(units[a], units[b])
            w[s] = new.astype(BF).reshape(w.shape[1:])

    def low_in(acts, unit):
        return mm_t(acts, units[unit]).astype(BF)

    def add_grad(unit, left, right):
        gacc[unit] += t_mm(left, right)

    x[:, :places, :] = tokens[...].astype(F32) + delta[...].astype(F32)
    up[:, :places, :] = cot[...].astype(F32) * valid[0, 0]

    xv = x[...].reshape(rows, width)
    n2 = (norm_parts(xv)[0] * gain_s[...]).astype(BF)
    n_lo[...] = n2
    for s in range(3):
        val = mm(n_lo[...], slab(s))
        if s == 0:
            val = val * HEAD ** (-0.5)
        split_lanes(qkv, s * lanes, val.astype(BF))

    def forward(i, carry):
        f = i // lanes
        hp = i % lanes
        r = pl.ds(f * pad, pad)
        p, o = attend(qkv[hp, r], qkv[lanes + hp, r], qkv[2 * lanes + hp, r], bias[...])
        probs[i] = p
        att[hp, r] = o
        return carry

    lax.fori_loop(0, chunk * lanes, forward, 0, unroll=2)

    heads = join_lanes(att, 0, lanes)
    ys[...] = x[...].reshape(rows, width) + mm_t(heads, slab(3))
    inner_so = low_in(heads, 4)
    n3 = (norm_parts(ys[...])[0] * gain_h[...]).astype(BF)
    n_lo[...] = n3
    inner_he = low_in(n3, 6)
    upl = up[...].reshape(rows, width).astype(BF)
    igrad_hr = mm_t(upl, units[15]).astype(BF)
    acc[...] = jnp.zeros_like(acc)
    dacc[...] = jnp.zeros_like(dacc)

    def feed(j, carry):
        inner_hr, igrad_he = carry
        hidden = mm(n_lo[...], w[4 + j].reshape(width, width))
        active, slope = gelu_parts(hidden)
        active = active.astype(BF)
        upl = up[...].reshape(rows, width).astype(BF)
        hgrad = (mm(upl, w[8 + j].reshape(width, width)) * slope).astype(BF)
        acc[...] += mm_t(active, w[8 + j].reshape(width, width))
        dacc[...] += mm_t(hgrad, w[4 + j].reshape(width, width))
        inner_hr = inner_hr + mm_t(active, units[11 + j])
        igrad_he = igrad_he + mm_t(hgrad, units[7 + j])
        gacc[11 + j] += t_mm(igrad_hr, active)
        gacc[7 + j] += t_mm(inner_he, hgrad)
        return (inner_hr, igrad_he)

    zero = jnp.zeros((rows, units.shape[1]), F32)
    inner_hr, igrad_he = lax.fori_loop(0, 4, feed, (zero, zero))
    add_grad(15, inner_hr.astype(BF), upl)
    add_grad(6, igrad_he.astype(BF), n_lo[...])

    res = (ys[...] + acc[...]) * valid[0, 0]
    out[...] = res.reshape(chunk, pad, width)[:, :places].astype(BF)
    sg = up[...].reshape(rows, width) + norm_back(dacc[...], ys[...], gain_h[...])
    acc[...] = sg
    sgl = sg.astype(BF)
    heads = join_lanes(att, 0, lanes)
    igrad = low_in(sgl, 5)
    add_grad(4, igrad, heads)
    add_grad(5, inner_so, sgl)
    split_lanes(att, 0, mm(sgl, slab(3)).astype(BF))

    def backward(i, carry):
        f = i // lanes
        hp = i % lanes
        r = pl.ds(f * pad, pad)
        dq, dk, dv = attend_back(
            att[hp, r], qkv[hp, r], qkv[lanes + hp, r], qkv[2 * lanes + hp, r], probs[i]
        )
        dqkv[hp, r] = dq
        dqkv[lanes + hp, r] = dk
        dqkv[2 * lanes + hp, r] = dv
        return carry

    lax.fori_loop(0, chunk * lanes, backward, 0, unroll=2)

    n2 = (norm_parts(x[...].reshape(rows, width))[0] * gain_s[...]).astype(BF)
    inner_sa = low_in(n2, 0)
    dn = jnp.zeros((rows, width), F32)
    igrad = jnp.zeros((rows, units.shape[1]), F32)
    for s in range(3):
        g = join_lanes(dqkv, s * lanes, lanes)
        dn = dn + mm_t(g, slab(s))
        igrad = igrad + mm_t(g, units[1 + s])
        add_grad(1 + s, inner_sa, g)
    add_grad(0, igrad.astype(BF), n2)
    tg = acc[...] + norm_back(dn, x[...].reshape(rows, width), gain_s[...])
    tg = tg.reshape(chunk, pad, width)[:, :places]
    tgrad[...] = tg
    tlow[...] = tg.astype(BF)

    @pl.when(step == pl.num_programs(0) - 1)
    def _():
        n, rank, _ = gacc.shape
        for c in range(lanes):
            grads[c] = gacc[:, :, c * 128 : c * 128 + 128].reshape(n * rank, 128).astype(BF)


def space_call(tokens, delta, cot, valid, gain_s, gain_h, units, gathered, chunk=2):
    frames, places, width = tokens.shape
    pad = -(-places // 16) * 16
    rows = chunk * pad
    nd, nt, count, wr, wc = gathered.shape
    n, rank, _ = units.shape
    lanes = width // 128
    block = pl.BlockSpec((chunk, places, width), lambda i: (i, 0, 0))
    full = lambda a: pl.BlockSpec(a.shape, lambda i: (0,) * a.ndim, pipeline_mode=pl.Buffered(1))
    return pl.pallas_call(
        partial(space_kernel, places=places, pad=pad),
        grid=(frames // chunk,),
        out_shape=(
            jax.ShapeDtypeStruct(tokens.shape, BF),
            jax.ShapeDtypeStruct(tokens.shape, F32),
            jax.ShapeDtypeStruct(tokens.shape, BF),
            jax.ShapeDtypeStruct((lanes, n * rank, 128), BF),
        ),
        in_specs=[
            block, block, block,
            pl.BlockSpec(memory_space=pltpu.SMEM),
            full(gain_s), full(gain_h), full(units),
            pl.BlockSpec(memory_space=pl.ANY),
        ],
        out_specs=(block, block, block, pl.BlockSpec((lanes, n * rank, 128), lambda i: (0, 0, 0))),
        scratch_shapes=[
            pltpu.VMEM((count, nd, wr, width), BF),
            pltpu.VMEM((chunk, pad, width), F32),
            pltpu.VMEM((chunk, pad, width), F32),
            pltpu.VMEM((rows, width), F32),
            pltpu.VMEM((rows, width), BF),
            pltpu.VMEM((3 * lanes, rows, 128), BF),
            pltpu.VMEM((3 * lanes, rows, 128), BF),
            pltpu.VMEM((chunk * lanes, 2 * pad, pad), BF),
            pltpu.VMEM((lanes, rows, 128), BF),
            pltpu.VMEM((rows, width), F32),
            pltpu.VMEM((rows, width), F32),
            pltpu.VMEM((n, rank, width), F32),
            pltpu.VMEM((pad, pad), F32),
            pltpu.SemaphoreType.DMA((count, nt)),
        ],
        compiler_params=pltpu.CompilerParams(
            dimension_semantics=("arbitrary",), vmem_limit_bytes=60 << 20
        ),
    )(tokens, delta, cot, valid, gain_s, gain_h, units, gathered)


TIME_SIDES = ((0, 1), (0, 2), (0, 3), (5, 4), (6, 7))


def load_weights(gathered, w, sems, units, sides):
    nd, nt, count, wr, wc = gathered.shape
    width = nt * wc
    moves = [
        [
            pltpu.make_async_copy(
                gathered.at[:, t, s], w.at[s, :, :, pl.ds(t * wc, wc)], sems.at[s, t]
            )
            for t in range(nt)
        ]
        for s in range(count)
    ]
    for pair in moves:
        for move in pair:
            move.start()
    for s in range(count):
        for move in moves[s]:
            move.wait()
        a, b = sides[s]
        new = w[s].reshape(width, width).astype(F32) + t_mm(units[a], units[b])
        w[s] = new.astype(BF).reshape(w.shape[1:])


def place_bias(bias, group):
    key = lax.broadcasted_iota(jnp.int32, bias.shape, 0)
    query = lax.broadcasted_iota(jnp.int32, bias.shape, 1)
    bias[...] = jnp.where(lax.rem(key, group) == lax.rem(query, group), 0.0, LOW)


def time_kernel(
    mine, got, gain, units, gathered,
    delta, qkv, probs, att, tout, w,
    x, n_lo, bias, sems,
    *, pad, group,
):
    nd, nt, count, wr, wc = gathered.shape
    width = nt * wc
    near, places, _ = mine.shape
    frames = near + got.shape[0]
    lanes = width // 128
    cut = frames // 2
    part = cut * pad
    size = frames * group
    load_weights(gathered, w, sems, units, TIME_SIDES)
    place_bias(bias, group)
    x[:near, :places, :] = mine[...].astype(F32)
    x[near:, :places, :] = got[...].astype(F32)
    x[:, places:, :] = jnp.zeros((frames, pad - places, width), F32)

    def slab(s):
        return w[s].reshape(width, width)

    def project(c, carry):
        r = pl.ds(c * cut, cut)
        n = (norm_parts(x[r].reshape(part, width))[0] * gain[...]).astype(BF)
        n_lo[...] = n
        for s in range(3):
            val = mm(n_lo[...], slab(s))
            if s == 0:
                val = val * HEAD ** (-0.5)
            val = val.astype(BF).reshape(cut, pad, width)
            for lane in range(lanes):
                qkv[s * lanes + lane, r] = val[:, :, lane * 128 : lane * 128 + 128]
        return carry

    lax.fori_loop(0, 2, project, 0)

    def forward(i, carry):
        b = i // lanes
        hp = i % lanes
        r = pl.ds(pl.multiple_of(b * group, group), group)
        q, k, v = [qkv[s * lanes + hp, :, r].reshape(size, 128) for s in range(3)]
        p, o = attend(q, k, v, bias[...])
        probs[i] = p
        att[hp, :, r] = o.reshape(frames, group, 128)
        return carry

    lax.fori_loop(0, (pad // group) * lanes, forward, 0, unroll=3)

    def merge(c, carry):
        r = pl.ds(c * cut, cut)
        heads = jnp.concatenate([att[lane, r].reshape(part, 128) for lane in range(lanes)], axis=-1)
        merged = mm_t(heads, slab(3)).astype(BF)
        tout[r] = merged.reshape(cut, pad, width)
        val = mm(merged, slab(4)).astype(BF)
        delta[r] = val.reshape(cut, pad, width)[:, :places]
        return carry

    lax.fori_loop(0, 2, merge, 0)


def time_call(mine, got, gain, units, gathered, group=16):
    near, places, width = mine.shape
    frames = 2 * near
    pad = -(-places // group) * group
    nd, nt, count, wr, wc = gathered.shape
    lanes = width // 128
    blocks = pad // group
    size = frames * group
    vm = pl.BlockSpec(memory_space=pltpu.VMEM)
    return pl.pallas_call(
        partial(time_kernel, pad=pad, group=group),
        out_shape=(
            jax.ShapeDtypeStruct((frames, places, width), BF),
            jax.ShapeDtypeStruct((3 * lanes, frames, pad, 128), BF),
            jax.ShapeDtypeStruct((blocks * lanes, 2 * size, size), BF),
            jax.ShapeDtypeStruct((lanes, frames, pad, 128), BF),
            jax.ShapeDtypeStruct((frames, pad, width), BF),
            jax.ShapeDtypeStruct((count, nd, wr, width), BF),
        ),
        in_specs=[vm, vm, vm, vm, pl.BlockSpec(memory_space=pl.ANY)],
        out_specs=(vm,) * 6,
        scratch_shapes=[
            pltpu.VMEM((frames, pad, width), F32),
            pltpu.VMEM((frames // 2 * pad, width), BF),
            pltpu.VMEM((size, size), F32),
            pltpu.SemaphoreType.DMA((count, nt)),
        ],
        compiler_params=pltpu.CompilerParams(vmem_limit_bytes=60 << 20),
    )(mine, got, gain, units, gathered)


def time_back_kernel(
    gmine, ggot, mine, got, gain, units, qkv, probs, att, tout, w,
    first, grads,
    x, g_lo, mg, dqkv, gacc,
    *, group,
):
    count, nd, wr, width = w.shape
    near, places, _ = mine.shape
    frames, pad, _ = tout.shape
    lanes = width // 128
    cut = frames // 2
    part = cut * pad
    size = frames * group
    gap = jnp.zeros((frames, pad - places, width), F32)
    x[:near, :places, :] = mine[...].astype(F32)
    x[near:, :places, :] = got[...].astype(F32)
    x[:, places:, :] = gap
    g_lo[:near, :places, :] = gmine[...]
    g_lo[near:, :places, :] = ggot[...]
    g_lo[:, places:, :] = gap.astype(BF)
    gacc[...] = jnp.zeros_like(gacc)

    def slab(s):
        return w[s].reshape(width, width)

    def flat(ref, r):
        return ref[r].reshape(part, width)

    def lane_rows(ref, base, r):
        return jnp.concatenate(
            [ref[base + lane, r].reshape(part, 128) for lane in range(lanes)], axis=-1
        )

    def outer(c, carry):
        r = pl.ds(c * cut, cut)
        g = flat(g_lo, r)
        merged = flat(tout, r)
        inner = mm_t(merged, units[6]).astype(BF)
        igrad = mm_t(g, units[7]).astype(BF)
        gacc[6] += t_mm(igrad, merged)
        gacc[7] += t_mm(inner, g)
        grad = mm_t(g, slab(4)).astype(BF)
        heads = lane_rows(att, 0, r)
        inner = mm_t(heads, units[4]).astype(BF)
        igrad = mm_t(grad, units[5]).astype(BF)
        gacc[4] += t_mm(igrad, heads)
        gacc[5] += t_mm(inner, grad)
        val = mm(grad, slab(3)).astype(BF).reshape(cut, pad, width)
        for lane in range(lanes):
            mg[lane, r] = val[:, :, lane * 128 : lane * 128 + 128]
        return carry

    lax.fori_loop(0, 2, outer, 0)

    def backward(i, carry):
        b = i // lanes
        hp = i % lanes
        r = pl.ds(pl.multiple_of(b * group, group), group)
        q, k, v = [qkv[s * lanes + hp, :, r].reshape(size, 128) for s in range(3)]
        g = mg[hp, :, r].reshape(size, 128)
        for s, val in enumerate(attend_back(g, q, k, v, probs[i])):
            dqkv[s * lanes + hp, :, r] = val.reshape(frames, group, 128)
        return carry

    lax.fori_loop(0, (pad // group) * lanes, backward, 0, unroll=3)

    def inner_part(c, carry):
        r = pl.ds(c * cut, cut)
        xv = flat(x, r)
        n = (norm_parts(xv)[0] * gain[...]).astype(BF)
        inner = mm_t(n, units[0]).astype(BF)
        dn = jnp.zeros((part, width), F32)
        igrad = jnp.zeros((part, units.shape[1]), F32)
        for s in range(3):
            g = lane_rows(dqkv, s * lanes, r)
            dn = dn + mm_t(g, slab(s))
            igrad = igrad + mm_t(g, units[1 + s])
            gacc[1 + s] += t_mm(inner, g)
        gacc[0] += t_mm(igrad.astype(BF), n)
        val = norm_back(dn, flat(x, r), gain[...]).astype(BF)
        first[r] = val.reshape(cut, pad, width)[:, :places]
        return carry

    lax.fori_loop(0, 2, inner_part, 0)
    n, rank, _ = gacc.shape
    for c in range(lanes):
        grads[c] = gacc[:, :, c * 128 : c * 128 + 128].reshape(n * rank, 128).astype(BF)


def time_back_call(gmine, ggot, mine, got, gain, units, qkv, probs, att, tout, w, group=16):
    near, places, width = mine.shape
    frames, pad, _ = tout.shape
    lanes = width // 128
    n, rank, _ = units.shape
    vm = pl.BlockSpec(memory_space=pltpu.VMEM)
    return pl.pallas_call(
        partial(time_back_kernel, group=group),
        out_shape=(
            jax.ShapeDtypeStruct((frames, places, width), BF),
            jax.ShapeDtypeStruct((lanes, n * rank, 128), BF),
        ),
        in_specs=[vm] * 11,
        out_specs=(vm, vm),
        scratch_shapes=[
            pltpu.VMEM((frames, pad, width), F32),
            pltpu.VMEM((frames, pad, width), BF),
            pltpu.VMEM((lanes, frames, pad, 128), BF),
            pltpu.VMEM((3 * lanes, frames, pad, 128), BF),
            pltpu.VMEM((n, rank, width), F32),
        ],
        compiler_params=pltpu.CompilerParams(vmem_limit_bytes=60 << 20),
    )(gmine, ggot, mine, got, gain, units, qkv, probs, att, tout, w)


ALL = ("dp", "tensor")


def body(
    tokens,
    cotangent,
    time_attend,
    time_output,
    time_mixing,
    space_attend,
    space_output,
    hidden_expand,
    hidden_reduce,
    norm_time,
    norm_space,
    norm_hidden,
    timeattend_lower,
    timeattend_raise,
    timeoutput_lower,
    timeoutput_raise,
    timemixing_lower,
    timemixing_raise,
    spaceattend_lower,
    spaceattend_raise,
    spaceoutput_lower,
    spaceoutput_raise,
    expand_lower,
    expand_raise,
    reduce_lower,
    reduce_raise,
    adapter_index,
    clip_mask,
    *,
    dp,
    tensor,
):
    me = lax.axis_index("tensor")
    devices = dp * tensor
    _, length, width = tokens.shape
    local = length // PLACES
    half = PLACES // tensor
    adapters, _, rank = timeattend_lower.shape
    cols = width // tensor
    pieces = hidden_expand.shape[1] // cols
    lanes = width // 128
    adapter = adapter_index[0]
    valid = clip_mask.astype(F32).reshape(1, 1)
    swap = [(i, (i + 1) % tensor) for i in range(tensor)]

    def slabs(matrix):
        return matrix.reshape(matrix.shape[0], -1, cols).transpose(1, 0, 2)

    def gather(pack):
        whole = lax.all_gather(pack, ALL, axis=0, tiled=False)
        count, rows, _ = pack.shape
        whole = whole.reshape(dp, tensor, count, rows, cols)
        if rows % 16:
            whole = whole.transpose(2, 0, 3, 1, 4).reshape(1, 1, count, width, width)
        return whole

    mixing_cols = lax.dynamic_slice_in_dim(time_mixing, me * cols, cols, 1)
    time_pack = [slabs(time_attend), slabs(time_output.T), slabs(mixing_cols)]
    rest_pack = [
        slabs(space_attend),
        slabs(space_output.T),
        slabs(hidden_expand),
        slabs(hidden_reduce.T),
    ]
    time_whole = gather(jnp.concatenate(time_pack, axis=0))
    rest_whole = gather(jnp.concatenate(rest_pack, axis=0))

    def pick(table):
        return lax.dynamic_index_in_dim(table, adapter, 0, keepdims=False)

    def lower(table):
        picked = pick(table)
        if picked.shape[0] == width:
            return picked.T[None]
        split = picked.reshape(tensor, pieces, cols, rank)
        return split.transpose(1, 3, 0, 2).reshape(pieces, rank, width)

    def raised(table):
        picked = pick(table)
        if picked.ndim == 3:
            return picked.transpose(1, 0, 2)
        if picked.shape[1] == width:
            return picked[None]
        split = picked.reshape(rank, tensor, pieces, cols)
        return split.transpose(2, 0, 1, 3).reshape(pieces, rank, width)

    time_tables = [
        lower(timeattend_lower),
        raised(timeattend_raise),
        lower(timeoutput_lower),
        raised(timeoutput_raise),
        lower(timemixing_lower),
        raised(timemixing_raise),
    ]
    rest_tables = [
        lower(spaceattend_lower),
        raised(spaceattend_raise),
        lower(spaceoutput_lower),
        raised(spaceoutput_raise),
        lower(expand_lower),
        raised(expand_raise),
        lower(reduce_lower),
        raised(reduce_raise),
    ]
    time_units = jnp.concatenate(time_tables, axis=0)
    rest_units = jnp.concatenate(rest_tables, axis=0)

    def to_places(values):
        mine = lax.dynamic_slice_in_dim(values, me * half, half, 1)
        other = lax.dynamic_slice_in_dim(values, (1 - me) * half, half, 1)
        return (mine, lax.ppermute(other, "tensor", swap))

    def to_frames(values):
        mine = values[:local]
        got = lax.ppermute(values[local:], "tensor", swap)
        first = jnp.where(me == 0, mine, got)
        second = jnp.where(me == 0, got, mine)
        return jnp.concatenate([first, second], axis=1)

    tokens = tokens.reshape(local, PLACES, width)
    cotangent = cotangent.reshape(local, PLACES, width)
    gains = [gain.reshape(1, width) for gain in (norm_time, norm_space, norm_hidden)]
    mine, got = to_places(tokens)
    delta, *kept = time_call(mine, got, gains[0], time_units, time_whole)
    layer_output, time_grad, time_low, late = space_call(
        tokens, to_frames(delta), cotangent, valid, gains[1], gains[2], rest_units, rest_whole
    )
    first, early = time_back_call(*to_places(time_low), mine, got, gains[0], time_units, *kept)
    input_grad = (time_grad + to_frames(first).astype(F32)).astype(BF)

    def reduce_tables(sums):
        flat = sums.reshape(-1, 128)
        each = flat.shape[0] // devices
        label = jnp.full((devices, 1, 128), adapter, jnp.int32).astype(BF)
        sent = jnp.concatenate([flat.reshape(devices, each, 128), label], axis=1)
        back = lax.all_to_all(sent, ALL, 0, 0, tiled=True)
        owner = back[:, each, :1].astype(jnp.int32)
        choose = (owner == jnp.arange(adapters, dtype=jnp.int32)[None, :]).astype(BF)
        total = lax.dot_general(
            choose, back[:, :each], (((0,), (0,)), ((), ())), preferred_element_type=F32
        )
        whole = lax.all_gather(total.astype(BF), ALL, axis=0, tiled=False)
        whole = whole.transpose(1, 0, 2, 3)
        return whole.reshape(adapters, lanes, -1, rank, 128)

    late = reduce_tables(late)
    early = reduce_tables(early)

    def lowered(part):
        if part.shape[2] == 1:
            return part[:, :, 0].transpose(0, 1, 3, 2).reshape(adapters, width, rank).astype(F32)
        whole = part.transpose(0, 3, 2, 1, 4).reshape(adapters, rank, pieces, tensor, cols)
        return whole.transpose(0, 3, 2, 4, 1).reshape(adapters, -1, rank).astype(F32)

    def wide(part):
        whole = part.transpose(0, 3, 2, 1, 4).reshape(adapters, rank, -1, width)
        return whole.astype(F32)

    def row(part):
        return wide(part).reshape(adapters, rank, width)

    expand = wide(late[:, :, 7:11]).reshape(adapters, rank, pieces, tensor, cols)
    expand = expand.transpose(0, 1, 3, 2, 4).reshape(adapters, rank, -1)
    return (
        layer_output.reshape(1, length, width),
        input_grad.reshape(1, length, width),
        lowered(early[:, :, 0:1]),
        wide(early[:, :, 1:4]),
        lowered(early[:, :, 4:5]),
        row(early[:, :, 5:6]),
        lowered(early[:, :, 6:7]),
        row(early[:, :, 7:8]),
        lowered(late[:, :, 0:1]),
        wide(late[:, :, 1:4]),
        lowered(late[:, :, 4:5]),
        row(late[:, :, 5:6]),
        lowered(late[:, :, 6:7]),
        expand,
        lowered(late[:, :, 11:15]),
        row(late[:, :, 15:16]),
    )


def solution(mesh):
    whole = P()
    step = partial(body, dp=mesh.shape["dp"], tensor=mesh.shape["tensor"])
    return jax.shard_map(
        step,
        mesh=mesh,
        in_specs=(
            P("dp", "tensor", None),
            P("dp", "tensor", None),
            P("dp", None, "tensor"),
            P("tensor", "dp"),
            P("dp", None),
            P("dp", None, "tensor"),
            P("tensor", "dp"),
            P("dp", "tensor"),
            P("tensor", "dp"),
        )
        + (whole,) * 17
        + (P("dp"), P("dp")),
        out_specs=(P("dp", "tensor", None), P("dp", "tensor", None)) + (whole,) * 14,
        check_vma=False,
    )
```

time: 758 us -> 498 us (0.66)
  matrix products: 212 us -> 1.59 us
  local copies, waits for them, and re-layouts: 241 us -> 65.6 us
  Pallas kernels: 0 us -> 146 us
  other arithmetic: 79.7 us -> 13.3 us
  blocking collectives: 0 us -> 29.2 us
  waiting for transfers between devices: 188 us -> 210 us
    dot_general x49 -> x2, matrix products: 212 us -> 1.59 us  [reduce_tables(): lax.dot_general(choose, back[:, :each], (((0,), (0,)), ((), ())), preferr...]
    pallas_call x0 -> x3, Pallas kernels: none -> 146 us  [the longest x1 86.3 us: space_call(): pl.pallas_call(partial(space_kernel, places=places, pad=pad), grid=(frame...]
    unnamed x253 -> x50, local copies, waits for them, and re-layouts: 65.2 us -> 12.3 us
    convert_element_type x16 -> x18, local copies, waits for them, and re-layouts: 62.4 us -> 17.4 us  [the longest x4 7.95 us: lowered(): whole.transpose(0, 3, 2, 4, 1).reshape(adapters, -1, rank).astype(F32)]
    all_gather x2, waiting for transfers between devices: 57.8 us -> 101 us  [gather(): whole = lax.all_gather(pack, ALL, axis=0, tiled=False)]
    reshape x30 -> x17, local copies, waits for them, and re-layouts: 55.9 us -> 14.3 us  [the longest x4 6.54 us: body(): expand = expand.transpose(0, 1, 3, 2, 4).reshape(adapters, rank, -1)]
    all_to_all x0 -> x2, blocking collectives: none -> 29.2 us  [reduce_tables(): back = lax.all_to_all(sent, ALL, 0, 0, tiled=True)]
    slice x22 -> x6, local copies, waits for them, and re-layouts: 31.3 us -> 3.32 us  [the longest x4 3.27 us: to_frames(): got = lax.ppermute(values[local:], 'tensor', swap)]
  transfers between devices with their start and end apart: 10 -> 8, of which waited for: 9 -> 8; matrix products, arithmetic and copies ran while one was open for 18% -> 9% of each run, Pallas kernels for 0% -> 6%
where the time goes in v1:
time: 498 us; the launch traced here: 490 us
  waiting for transfers between devices  210 us (42%)
  Pallas kernels  146 us (29%)
  local copies, waits for them, and re-layouts  65.6 us (13%)
  blocking collectives  29.2 us (6%)
  between operations  15.7 us (3%)
  other arithmetic  13.3 us (3%)
  starting transfers between devices  7.93 us (2%)
    all_gather x2, waiting for transfers between devices, gather(): whole = lax.all_gather(pack, ALL, axis=0, tiled=False)  101 us
    pallas_call x1, Pallas kernels, space_call(): pl.pallas_call(partial(space_kernel, places=places, pad=pad), grid=(frame...  86.3 us
    all_gather x2, waiting for transfers between devices, reduce_tables(): whole = lax.all_gather(total.astype(BF), ALL, axis=0, tiled=False)  63.9 us
    pallas_call x1, Pallas kernels, time_back_call(): pl.pallas_call(partial(time_back_kernel, group=group), out_shape=(jax.Sha...  32.5 us
    all_to_all x2, blocking collectives, reduce_tables(): back = lax.all_to_all(sent, ALL, 0, 0, tiled=True)  29.2 us
    pallas_call x1, Pallas kernels, time_call(): pl.pallas_call(partial(time_kernel, pad=pad, group=group), out_shape=(jax...  27.7 us
    ppermute x2, waiting for transfers between devices, to_frames(): got = lax.ppermute(values[local:], 'tensor', swap)  24.7 us
    ppermute x2, waiting for transfers between devices, to_places(): return (mine, lax.ppermute(other, 'tensor', swap))  20.3 us
  transfers between devices with their start and end apart: 8, of which 8 were waited for; matrix products, arithmetic and copies ran while one was open for 9% of the time, Pallas kernels for 6%

profile of v1, /device:TPU:0, one launch (start us, length us, event | category | flops | bytes accessed | tf_op | source)
XLA Modules:
  0.0 489.9 jit_solution(13138489511304167423)
XLA Ops:
  8.1 1.6 pad_maximum_fusion.2
  15.9 3.0 collective-permute-start
  22.3 1.6 bitcast_dynamic-update-slice_fusion
  27.8 6.1 %collective-permute-done = bf16[4,98,768]{2,0,1:T(4,128)(2,1)S(1)} collective-permute-done((bf16[4,98,768]{2,0,1:T(4,128)(2,1)S(1)}, bf16[4,98,768]{2,0,1:T(4,128)(2,1)S(1)}, u32[]{:S(2)}, u32[]{:S(2)}) %collective-permute-start) | collective-permute-done | bytes 602144 | tf_op jit(solution)/shard_map/ppermute | solution.py:646
  34.7 48.3 %all-gather.9.cloned.1.call-done = bf16[160,48,384]{2,1,0:T(8,128)(2,1)} async-done(((bf16[5,48,384]{2,1,0:T(8,128)(2,1)}), bf16[160,48,384]{2,1,0:T(8,128)(2,1)}) %all-gather.9.cloned.1.call-update) | async-done | bytes 5898256 | tf_op jit(solution)/shard_map/all_gather | solution.py:585
  83.0 27.7 %shard_map.387 = (bf16[8,98,768]{2,1,0:T(8,128)(2,1)}, bf16[18,8,112,128]{3,2,1,0:T(8,128)(2,1)}, bf16[42,256,128]{2,1,0:T(8,128)(2,1)}, bf16[6,8,112,128]{3,2,1...) custom-call(bf16[4,98,768]{2,1,0:T(8,128)(2,1)} %get-tuple-element.59.mine, ...), custom_call_target="tpu_custom_call" | custom-call | tf_op jit(solution)/shard_map/pallas_call | solution.py:396
  112.9 1.5 collective-permute-start.1
  119.2 1.4 constant_dynamic-update-slice_fusion.9
  124.5 10.8 %collective-permute-done.1 = bf16[4,98,768]{2,0,1:T(4,128)(2,1)} collective-permute-done((bf16[4,98,768]{2,0,1:T(4,128)(2,1)}, bf16[4,98,768]{2,0,1:T(4,128)(2,1)}, u32[]{:S(2)}, u32[]{:S(2)}) %collective-permute-start.1) | collective-permute-done | bytes 602144 | tf_op jit(solution)/shard_map/ppermute | solution.py:650
  137.7 52.8 %all-gather.11.cloned.1.call-done = bf16[384,48,384]{2,1,0:T(8,128)(2,1)} async-done(((bf16[12,48,384]{2,1,0:T(8,128)(2,1)}), bf16[384,48,384]{2,1,0:T(8,128)(2,1)}) %all-gather.11.cloned.1.call-update) | async-done | bytes 14155792 | tf_op jit(solution)/shard_map/all_gather | solution.py:585
  190.6 86.3 %shard_map.388 = (bf16[4,196,768]{2,1,0:T(8,128)(2,1)}, f32[4,196,768]{2,1,0:T(8,128)}, bf16[4,196,768]{2,1,0:T(8,128)(2,1)}, bf16[6,256,128]{2,1,0:T(8,128)(2,1)}) custom-call(bf16[4,196,768]{2,1,0:T(8,128)(2,1)} %copy-done.2, bf16[4,196,768]{2,1,0:T(8,128)(2,1)} %pad_maximum_fusion.delta, bf16[4,196,768]{2,1,0:T(8,128)(2,1)} %reshape.194.cot, ...), custom_call_target="tpu_custom_call" | custom-call | tf_op jit(solution)/shard_map/pallas_call | solution.py:255
  276.9 2.4 constant_dynamic-slice_fusion
  279.6 1.5 collective-permute-start.2
  281.1 14.3 %collective-permute-done.2 = bf16[4,98,768]{2,0,1:T(4,128)(2,1)S(1)} collective-permute-done((bf16[4,98,768]{2,0,1:T(4,128)(2,1)S(1)}, bf16[4,98,768]{2,0,1:T(4,128)(2,1)S(1)}, u32[]{:S(2)}, u32[]{:S(2)}) %collective-permute-start.2) | collective-permute-done | bytes 602144 | tf_op jit(solution)/shard_map/ppermute | solution.py:646
  296.3 32.5 %shard_map.389 = (bf16[8,98,768]{2,1,0:T(8,128)(2,1)}, bf16[6,128,128]{2,1,0:T(8,128)(2,1)}) custom-call(bf16[4,98,768]{2,1,0:T(8,128)(2,1)} %get-tuple-element.57.gmine, bf16[4,98,768]{2,1,0:T(8,128)(2,1)} %copy.177.ggot, bf16[4,98,768]{2,1,0:T(8,128)(2,1)} %get-tuple-element.59.mine, bf16[4,98,768]{2,1,0:T(8,128)(2,1)} %copy.167.got, ...), custom_call_target="tpu_custom_call" | custom-call | tf_op jit(solution)/shard_map/pallas_call | solution.py:513
  329.8 13.2 %all_to_all.10 = bf16[32,25,128]{2,1,0:T(8,128)(2,1)S(1)} all-to-all(bf16[32,25,128]{2,1,0:T(8,128)(2,1)S(1)} %concatenate.30), channel_id=1, replica_groups=mesh['dp'=16,'tensor'=2] {'dp','tensor'}, dimensions={0} | all-to-all | bytes 409600 | tf_op jit(solution)/shard_map/all_to_all | solution.py:671
  344.6 16.0 %all_to_all.11 = bf16[32,49,128]{2,1,0:T(8,128)(2,1)S(1)} all-to-all(bf16[32,49,128]{2,1,0:T(8,128)(2,1)S(1)} %concatenate.31), channel_id=1, replica_groups=mesh['dp'=16,'tensor'=2] {'dp','tensor'}, dimensions={0} | all-to-all | bytes 802816 | tf_op jit(solution)/shard_map/all_to_all | solution.py:671
  363.2 1.7 collective-permute-start.3
  366.1 13.9 %collective-permute-done.3 = bf16[4,98,768]{2,0,1:T(4,128)(2,1)} collective-permute-done((bf16[4,98,768]{2,0,1:T(4,128)(2,1)}, bf16[4,98,768]{2,0,1:T(4,128)(2,1)}, u32[]{:S(2)}, u32[]{:S(2)}) %collective-permute-start.3) | collective-permute-done | bytes 602144 | tf_op jit(solution)/shard_map/ppermute | solution.py:650
  382.9 11.8 %all-gather.13.cloned.1.call-done = bf16[256,24,128]{2,0,1:T(8,128)(2,1)} async-done(((bf16[8,24,128]{2,0,1:T(8,128)(2,1)}), bf16[256,24,128]{2,0,1:T(8,128)(2,1)}) %all-gather.13.cloned.1.call-update) | async-done | bytes 1572880 | tf_op jit(solution)/shard_map/all_gather | solution.py:677
  394.7 2.4 copy.183
  400.1 1.8 copy.232
  404.5 52.1 %all-gather.15.cloned.1.call-done = bf16[256,48,128]{2,0,1:T(8,128)(2,1)} async-done(((bf16[8,48,128]{2,0,1:T(8,128)(2,1)}), bf16[256,48,128]{2,0,1:T(8,128)(2,1)}) %all-gather.15.cloned.1.call-update) | async-done | bytes 3145744 | tf_op jit(solution)/shard_map/all_gather | solution.py:677
  456.6 3.9 copy.191
  460.5 1.4 convert_bitcast_fusion
  465.2 2.0 reshape.236
  467.3 1.8 copy.198
  469.1 1.8 reshape.225
  470.9 2.3 copy.199
  473.2 2.0 reshape.237
  475.2 1.8 copy.200
  477.1 1.8 reshape.226
  (118 shorter events, 50.6 us)
Async XLA Ops:
  7.2 19.6 %copy-start = (bf16[8,16,3072]{2,1,0:T(8,128)(2,1)S(1)}, bf16[8,16,3072]{2,1,0:T(8,128)(2,1)}, u32[]{:S(2)}) copy-start(bf16[8,16,3072]{2,1,0:T(8,128)(2,1)} %param.51) | copy-start | bytes 2359300
  7.2 5.5 %copy-start.15 = (bf16[384,48]{0,1:T(8,128)(2,1)S(1)}, bf16[384,48]{0,1:T(8,128)(2,1)}, u32[]{:S(2)}) copy-start(bf16[384,48]{0,1:T(8,128)(2,1)} %param.34) | copy-start | bytes 110596
  7.2 75.8 %all-gather.9.cloned.1.call-start = ((), (), s32[]{:S(2)}) async-start(), calls=%async_computation.2 | async-start | bytes 6082560 | tf_op jit(solution)/shard_map/all_gather | solution.py:585
  9.7 180.8 %all-gather.11.cloned.1.call-start = ((), (), s32[]{:S(2)}) async-start(), calls=%async_computation.3 | async-start | bytes 14598144 | tf_op jit(solution)/shard_map/all_gather | solution.py:585
  12.7 1.5 copy-start.11
  14.1 380.6 %all-gather.13.cloned.1.call-start = ((), (), s32[]{:S(2)}) async-start(), calls=%async_computation.4 | async-start | bytes 1622016 | tf_op jit(solution)/shard_map/all_gather | solution.py:677
  14.4 1.5 copy-start.2
  14.4 5.2 %copy-start.16 = (f32[768]{0:T(1024)S(1)}, f32[768]{0:T(1024)}, u32[]{:S(2)}) copy-start(f32[768]{0:T(1024)} %param.37) | copy-start | bytes 9220
  15.9 17.9 %collective-permute-start = (bf16[4,98,768]{2,0,1:T(4,128)(2,1)S(1)}, bf16[4,98,768]{2,0,1:T(4,128)(2,1)S(1)}, u32[]{:S(2)}, u32[]{:S(2)}) collective-permute-start(bf16[4,98,768]{2,0,1:T(4,128)(2,1)S(1)} %copy.166), channel_id=1, source_target_pairs={{0,1},{1,0},{2,3},{3,2},{4,5},{5,4},{6,7},{7,6},{8,9},{9,8},{10,11... | collective-permute-start | bytes 1806344 | tf_op jit(solution)/shard_map/ppermute | solution.py:646
  26.8 56.2 %copy-start.13 = (bf16[8,16,768]{2,1,0:T(8,128)(2,1)}, bf16[8,16,768]{2,1,0:T(8,128)(2,1)S(1)}, u32[]{:S(2)}) copy-start(bf16[8,16,768]{2,1,0:T(8,128)(2,1)S(1)} %constant_dynamic-update-slice_fusion.units) | copy-start | bytes 589828
  111.8 4.3 copy-start.12
  112.9 22.4 %collective-permute-start.1 = (bf16[4,98,768]{2,0,1:T(4,128)(2,1)}, bf16[4,98,768]{2,0,1:T(4,128)(2,1)}, u32[]{:S(2)}, u32[]{:S(2)}) collective-permute-start(bf16[4,98,768]{2,0,1:T(4,128)(2,1)} %copy.168), channel_id=1, source_target_pairs={{0,1},{1,0},{2,3},{3,2},{4,5},{5,4},{6,7},{7,6},{8,9},{9,8},{10,11... | collective-permute-start | bytes 1806344 | tf_op jit(solution)/shard_map/ppermute | solution.py:650
  116.0 1.4 copy-start.17
  116.0 2.0 copy-start.18
  116.2 19.2 %copy-start.9 = (bf16[8,98,768]{2,1,0:T(8,128)(2,1)S(1)}, bf16[8,98,768]{2,1,0:T(8,128)(2,1)}, u32[]{:S(2)}) copy-start(bf16[8,98,768]{2,1,0:T(8,128)(2,1)} %get-tuple-element.28) | copy-start | bytes 3612676
  279.6 15.8 %collective-permute-start.2 = (bf16[4,98,768]{2,0,1:T(4,128)(2,1)S(1)}, bf16[4,98,768]{2,0,1:T(4,128)(2,1)S(1)}, u32[]{:S(2)}, u32[]{:S(2)}) collective-permute-start(bf16[4,98,768]{2,0,1:T(4,128)(2,1)S(1)} %copy.176), channel_id=1, source_target_pairs={{0,1},{1,0},{2,3},{3,2},{4,5},{5,4},{6,7},{7,6},{8,9},{9,8},{10,11... | collective-permute-start | bytes 1806344 | tf_op jit(solution)/shard_map/ppermute | solution.py:646
  328.8 15.8 %copy-start.14 = (bf16[6,256,128]{2,1,0:T(8,128)(2,1)S(1)}, bf16[6,256,128]{2,1,0:T(8,128)(2,1)}, u32[]{:S(2)}) copy-start(bf16[6,256,128]{2,1,0:T(8,128)(2,1)} %get-tuple-element.39) | copy-start | bytes 1179652
  344.5 112.1 %all-gather.15.cloned.1.call-start = ((), (), s32[]{:S(2)}) async-start(), calls=%async_computation.5 | async-start | bytes 3244032 | tf_op jit(solution)/shard_map/all_gather | solution.py:677
  344.6 17.6 %copy-start.8 = (bf16[8,98,768]{2,1,0:T(8,128)(2,1)S(1)}, bf16[8,98,768]{2,1,0:T(8,128)(2,1)}, u32[]{:S(2)}) copy-start(bf16[8,98,768]{2,1,0:T(8,128)(2,1)} %get-tuple-element.37) | copy-start | bytes 3612676
  362.1 2.9 copy-start.10
  363.2 16.7 %collective-permute-start.3 = (bf16[4,98,768]{2,0,1:T(4,128)(2,1)}, bf16[4,98,768]{2,0,1:T(4,128)(2,1)}, u32[]{:S(2)}, u32[]{:S(2)}) collective-permute-start(bf16[4,98,768]{2,0,1:T(4,128)(2,1)} %copy.179), channel_id=1, source_target_pairs={{0,1},{1,0},{2,3},{3,2},{4,5},{5,4},{6,7},{7,6},{8,9},{9,8},{10,11... | collective-permute-start | bytes 1806344 | tf_op jit(solution)/shard_map/ppermute | solution.py:650
  366.1 15.1 %copy-start.3 = (f32[4,196,768]{2,1,0:T(8,128)S(1)}, f32[4,196,768]{2,1,0:T(8,128)}, u32[]{:S(2)}) copy-start(f32[4,196,768]{2,1,0:T(8,128)} %get-tuple-element.30) | copy-start | bytes 7225348
  477.1 1.8 copy-start.4
  479.0 1.8 copy-start.7
  479.8 1.8 copy-start.6
  480.0 2.4 copy-start.5
  480.0 3.2 copy-start.1
Sparse Core Ops, SparseCore 0:
  11.5 71.4 all-gather.8
  86.5 104.0 all-gather.10
  344.6 50.0 all-gather.12
  398.0 58.5 all-gather.14
